TPU v7x, 32 devices: a whole 2x2x4 slice. The times are simulated.
32 devices in a mesh: ctx: 8 (over z, y), fsdp: 4 (over x, core).
Axes of the slice: x: 2, y: 2, z: 4, core: 2. Of those that a mesh axis runs over, the one named last changes fastest.
Arguments:
- tokens: bfloat16 [4, 1024, 768], P('fsdp', 'ctx'), may hold values from -6 to 6
- first_gain: bfloat16 [768], P('fsdp'), may hold values from 0.5 to 1.5
- first_bias: bfloat16 [768], P('fsdp'), may hold values from -4 to 4
- attn_weight: bfloat16 [768, 2304], P('fsdp'), may hold values from -0.3125 to 0.3125
- query_bias: bfloat16 [768], P('fsdp'), may hold values from -4 to 4
- value_bias: bfloat16 [768], P('fsdp'), may hold values from -4 to 4
- proj_weight: bfloat16 [768, 768], P('fsdp'), may hold values from -6 to 6
- proj_bias: bfloat16 [768], P('fsdp'), may hold values from -6 to 6
- second_gain: bfloat16 [768], P('fsdp'), may hold values from 0.5 to 1.5
- second_bias: bfloat16 [768], P('fsdp'), may hold values from -4 to 4
- fc_weight: bfloat16 [768, 3072], P('fsdp'), may hold values from -0.21875 to 0.21875
- fc_bias: bfloat16 [3072], P('fsdp'), may hold values from -6 to 6
- out_weight: bfloat16 [3072, 768], P('fsdp'), may hold values from -0.3125 to 0.3125
- out_bias: bfloat16 [768], P('fsdp'), may hold values from -6 to 6
- cotangent: bfloat16 [4, 1024, 768], P('fsdp', 'ctx'), may hold values from -6 to 6
Outputs:
- block_out: bfloat16 [4, 1024, 768], P('fsdp', 'ctx')
- input_grad: bfloat16 [4, 1024, 768], P('fsdp', 'ctx')
- first_gain_grad: float32 [768], P('fsdp')
- first_bias_grad: float32 [768], P('fsdp')
- attn_weight_grad: float32 [768, 2304], P('fsdp')
- query_bias_grad: float32 [768], P('fsdp')
- value_bias_grad: float32 [768], P('fsdp')
- proj_weight_grad: float32 [768, 768], P('fsdp')
- proj_bias_grad: float32 [768], P('fsdp')
- second_gain_grad: float32 [768], P('fsdp')
- second_bias_grad: float32 [768], P('fsdp')
- fc_weight_grad: float32 [768, 3072], P('fsdp')
- fc_bias_grad: float32 [3072], P('fsdp')
- out_weight_grad: float32 [3072, 768], P('fsdp')
- out_bias_grad: float32 [768], P('fsdp')
All inputs are finite; a program needn't handle non-finite values.
Results may differ from a plain program's by a relative error of at most 0.017.
Values may be sent and summed in bfloat16 or wider, within the bound.
No kernel may reach another device: no remote copies, remote signals or barrier semaphores. Data moves between devices by JAX's collectives and lax.ppermute only.
A program may use at most 320 MiB of HBM per device.

v0:
```python
from functools import partial
import jax
import jax.numpy as jnp
from jax import lax
from jax.sharding import PartitionSpec as P

D = 768
H = 12
HD = 64
LAYERS = 12
EPSILON = 1e-05


def layer_norm(values_in, norm_gain, norm_shift):
    center = jnp.mean(values_in, axis=-1, keepdims=True)
    centered = values_in - center
    spread = jnp.mean(centered * centered, axis=-1, keepdims=True)
    return centered * lax.rsqrt(spread + EPSILON) * norm_gain + norm_shift


def left_product(first, second):
    return lax.dot_general(
        first, second, (((0,), (0,)), ((), ())), preferred_element_type=jnp.float32
    )


def right_product(first, second):
    return lax.dot_general(
        first, second, (((1,), (1,)), ((), ())), preferred_element_type=jnp.float32
    )


def score_block(query_rows, key_rows, query_offset, key_offset):
    scores = jnp.einsum(
        "sqhd,skhd->shqk", query_rows, key_rows, preferred_element_type=jnp.float32
    ) * HD ** (-0.5)
    query_index = query_offset + lax.broadcasted_iota(jnp.int32, (query_rows.shape[1], 1), 0)
    key_index = key_offset + lax.broadcasted_iota(jnp.int32, (1, key_rows.shape[1]), 1)
    return (scores, (key_index <= query_index)[None, None])


def pair_terms(
    query_rows, grad_rows, log_totals, deltas, key_rows, value_rows, query_offset, key_offset
):
    scores, visible = score_block(query_rows, key_rows, query_offset, key_offset)
    weights = jnp.where(visible, jnp.exp(scores - log_totals[..., None]), 0.0)
    grad_weights = jnp.einsum(
        "sqhd,skhd->shqk", grad_rows, value_rows, preferred_element_type=jnp.float32
    )
    grad_scores = (weights * (grad_weights - deltas[..., None])).astype(jnp.bfloat16)
    return (weights.astype(jnp.bfloat16), grad_scores)


def shards(
    tokens,
    first_gain,
    first_bias,
    attn_weight,
    query_bias,
    value_bias,
    proj_weight,
    proj_bias,
    second_gain,
    second_bias,
    fc_weight,
    fc_bias,
    out_weight,
    out_bias,
    cotangent,
):
    residual_scale = LAYERS ** (-0.5)
    score_scale = HD ** (-0.5)
    seq_count = tokens.shape[0]
    block_rows = tokens.shape[1]
    all_rows = seq_count * block_rows
    inputs = tokens.reshape(all_rows, D).astype(jnp.float32)
    ctx_index = lax.axis_index("ctx")
    my_offset = ctx_index * block_rows
    last_row = my_offset + block_rows - 1
    attn_gathered = (
        lax.all_gather(first_gain, "fsdp", axis=0, tiled=True),
        lax.all_gather(first_bias, "fsdp", axis=0, tiled=True),
        lax.all_gather(attn_weight, "fsdp", axis=0, tiled=True),
        lax.all_gather(query_bias, "fsdp", axis=0, tiled=True),
        lax.all_gather(value_bias, "fsdp", axis=0, tiled=True),
        lax.all_gather(proj_weight, "fsdp", axis=0, tiled=True),
        lax.all_gather(proj_bias, "fsdp", axis=0, tiled=True),
    )
    gain_one, shift_one, attn_matrix, query_shift, value_shift, proj_matrix, proj_shift = (
        attn_gathered
    )
    gain_one = gain_one.astype(jnp.float32)
    shift_one = shift_one.astype(jnp.float32)
    normed = layer_norm(inputs, gain_one, shift_one).astype(jnp.bfloat16)
    mixed_rows = jnp.dot(normed, attn_matrix, preferred_element_type=jnp.float32)
    query_flat = (
        (mixed_rows[:, :D] + query_shift.astype(jnp.float32))
        .astype(jnp.bfloat16)
        .reshape(seq_count, block_rows, D)
    )
    key_flat = mixed_rows[:, D : 2 * D].astype(jnp.bfloat16).reshape(seq_count, block_rows, D)
    value_flat = (
        (mixed_rows[:, 2 * D :] + value_shift.astype(jnp.float32))
        .astype(jnp.bfloat16)
        .reshape(seq_count, block_rows, D)
    )
    query_heads = query_flat.reshape(seq_count, block_rows, H, HD)
    start_state = (
        jnp.full((seq_count, H, block_rows), -1e30, jnp.float32),
        jnp.zeros((seq_count, H, block_rows), jnp.float32),
        jnp.zeros((seq_count, H, block_rows, HD), jnp.float32),
    )
    offset = jnp.int32(0)
    key_rows = lax.all_gather(key_flat, "ctx", axis=1, tiled=True)
    value_rows = lax.all_gather(value_flat, "ctx", axis=1, tiled=True)
    row_count = key_rows.shape[1]

    def update(running):
        running_max, running_sum, running_acc = running
        scores, visible = score_block(
            query_heads, key_rows.reshape(seq_count, row_count, H, HD), my_offset, offset
        )
        scores = jnp.where(visible, scores, -1e30)
        new_max = jnp.maximum(running_max, jnp.max(scores, axis=-1))
        weights = jnp.where(visible, jnp.exp(scores - new_max[..., None]), 0.0)
        running_acc = jnp.einsum(
            "shqk,skhd->shqd",
            weights.astype(jnp.bfloat16),
            value_rows.reshape(seq_count, row_count, H, HD),
            preferred_element_type=jnp.float32,
        )
        running_sum = jnp.sum(weights, axis=-1)
        return (new_max, running_sum, running_acc)

    final_max, final_sum, final_acc = lax.cond(
        offset <= last_row, update, lambda unchanged: unchanged, start_state
    )
    log_totals = final_max + jnp.log(final_sum)
    attended_heads = final_acc / final_sum[..., None]
    attended_exact = attended_heads.transpose(0, 2, 1, 3).reshape(all_rows, D)
    attended = attended_exact.astype(jnp.bfloat16)
    branch = jnp.dot(attended, proj_matrix, preferred_element_type=jnp.float32) + proj_shift.astype(
        jnp.float32
    )
    middle = inputs + residual_scale * branch
    mlp_gathered = (
        lax.all_gather(second_gain, "fsdp", axis=0, tiled=True),
        lax.all_gather(second_bias, "fsdp", axis=0, tiled=True),
        lax.all_gather(fc_weight, "fsdp", axis=0, tiled=True),
        lax.all_gather(fc_bias, "fsdp", axis=0, tiled=True),
        lax.all_gather(out_weight, "fsdp", axis=0, tiled=True),
        lax.all_gather(out_bias, "fsdp", axis=0, tiled=True),
    )
    gain_two, shift_two, fc_matrix, fc_shift, out_matrix, out_shift = mlp_gathered
    gain_two = gain_two.astype(jnp.float32)
    shift_two = shift_two.astype(jnp.float32)
    normed_two = layer_norm(middle, gain_two, shift_two).astype(jnp.bfloat16)
    hidden = jnp.dot(normed_two, fc_matrix, preferred_element_type=jnp.float32) + fc_shift.astype(
        jnp.float32
    )
    gelu_fn = partial(jax.nn.gelu, approximate=True)
    active_exact, gelu_back = jax.vjp(gelu_fn, hidden)
    active = active_exact.astype(jnp.bfloat16)
    output = jnp.dot(active, out_matrix, preferred_element_type=jnp.float32) + out_shift.astype(
        jnp.float32
    )
    block_out = (middle + residual_scale * output).astype(jnp.bfloat16)
    grad_rows = cotangent.reshape(all_rows, D).astype(jnp.float32)
    grad_output = (residual_scale * grad_rows).astype(jnp.bfloat16)
    out_weight_grad = left_product(active, grad_output)
    out_bias_grad = jnp.sum(grad_output.astype(jnp.float32), axis=0)
    grad_active = right_product(grad_output, out_matrix)
    grad_hidden = gelu_back(grad_active)[0].astype(jnp.bfloat16)
    fc_weight_grad = left_product(normed_two, grad_hidden)
    fc_bias_grad = jnp.sum(grad_hidden.astype(jnp.float32), axis=0)
    grad_normed_two = right_product(grad_hidden, fc_matrix)
    norm_two_value, norm_two_back = jax.vjp(layer_norm, middle, gain_two, shift_two)
    grad_middle, second_gain_grad, second_bias_grad = norm_two_back(grad_normed_two)
    grad_middle = grad_middle + grad_rows
    grad_branch = (residual_scale * grad_middle).astype(jnp.bfloat16)
    proj_weight_grad = left_product(attended, grad_branch)
    proj_bias_grad = jnp.sum(grad_branch.astype(jnp.float32), axis=0)
    grad_attended = right_product(grad_branch, proj_matrix).astype(jnp.bfloat16)
    grad_heads = grad_attended.reshape(seq_count, block_rows, H, HD)
    grad_seq = grad_attended.reshape(seq_count, block_rows, D)
    deltas = jnp.sum(grad_heads.astype(jnp.float32).transpose(0, 2, 1, 3) * attended_heads, axis=-1)
    zero_flat = jnp.zeros((seq_count, block_rows, D), jnp.float32)
    zero_heads = jnp.zeros((seq_count, block_rows, H, HD), jnp.float32)
    all_totals, all_deltas = (
        lax.all_gather(log_totals, "ctx", axis=2, tiled=True),
        lax.all_gather(deltas, "ctx", axis=2, tiled=True),
    )
    key_heads_own = key_flat.reshape(seq_count, block_rows, H, HD)
    value_heads_own = value_flat.reshape(seq_count, block_rows, H, HD)

    def key_side(carried, arrived, offset):
        query_rows, grad_piece = arrived
        row_count = query_rows.shape[1]

        def key_visit_block(partials):
            query_part = query_rows.reshape(seq_count, row_count, H, HD)
            grad_part = grad_piece.reshape(seq_count, row_count, H, HD)
            weights, grad_scores = pair_terms(
                query_part,
                grad_part,
                all_totals,
                all_deltas,
                key_heads_own,
                value_heads_own,
                offset,
                my_offset,
            )
            key_sum = score_scale * jnp.einsum(
                "shqk,sqhd->skhd", grad_scores, query_part, preferred_element_type=jnp.float32
            ).reshape(seq_count, block_rows, D)
            value_sum = jnp.einsum(
                "shqk,sqhd->skhd", weights, grad_part, preferred_element_type=jnp.float32
            ).reshape(seq_count, block_rows, D)
            return (key_sum, value_sum)

        return lax.cond(
            offset + row_count - 1 >= my_offset,
            key_visit_block,
            lambda unchanged: unchanged,
            carried,
        )

    key_grad, value_grad = key_side(
        (zero_flat, zero_flat),
        (
            lax.all_gather(query_flat, "ctx", axis=1, tiled=True),
            lax.all_gather(grad_seq, "ctx", axis=1, tiled=True),
        ),
        jnp.int32(0),
    )

    def query_side(carried, arrived, offset):
        key_rows, value_rows = arrived
        row_count = key_rows.shape[1]

        def query_visit_block(query_sum):
            key_part = key_rows.reshape(seq_count, row_count, H, HD)
            weights, grad_scores = pair_terms(
                query_heads,
                grad_heads,
                log_totals,
                deltas,
                key_part,
                value_rows.reshape(seq_count, row_count, H, HD),
                my_offset,
                offset,
            )
            return score_scale * jnp.einsum(
                "shqk,skhd->sqhd", grad_scores, key_part, preferred_element_type=jnp.float32
            )

        return lax.cond(offset <= last_row, query_visit_block, lambda unchanged: unchanged, carried)

    query_grad = query_side(
        zero_heads,
        (
            lax.all_gather(key_flat, "ctx", axis=1, tiled=True),
            lax.all_gather(value_flat, "ctx", axis=1, tiled=True),
        ),
        jnp.int32(0),
    )
    grad_mixed = jnp.concatenate(
        [
            query_grad.reshape(all_rows, D).astype(jnp.bfloat16),
            key_grad.reshape(all_rows, D).astype(jnp.bfloat16),
            value_grad.reshape(all_rows, D).astype(jnp.bfloat16),
        ],
        axis=1,
    )
    attn_weight_grad = left_product(normed, grad_mixed)
    query_bias_grad = jnp.sum(grad_mixed[:, :D].astype(jnp.float32), axis=0)
    value_bias_grad = jnp.sum(grad_mixed[:, 2 * D :].astype(jnp.float32), axis=0)
    grad_normed = right_product(grad_mixed, attn_matrix)
    norm_one_value, norm_one_back = jax.vjp(layer_norm, inputs, gain_one, shift_one)
    grad_inputs, first_gain_grad, first_bias_grad = norm_one_back(grad_normed)
    input_grad = (grad_inputs + grad_middle).astype(jnp.bfloat16)
    owned = (
        lax.psum_scatter(
            first_gain_grad.astype(jnp.bfloat16), "fsdp", scatter_dimension=0, tiled=True
        ).astype(jnp.float32),
        lax.psum_scatter(
            first_bias_grad.astype(jnp.bfloat16), "fsdp", scatter_dimension=0, tiled=True
        ).astype(jnp.float32),
        lax.psum_scatter(
            attn_weight_grad.astype(jnp.bfloat16), "fsdp", scatter_dimension=0, tiled=True
        ).astype(jnp.float32),
        lax.psum_scatter(
            query_bias_grad.astype(jnp.bfloat16), "fsdp", scatter_dimension=0, tiled=True
        ).astype(jnp.float32),
        lax.psum_scatter(
            value_bias_grad.astype(jnp.bfloat16), "fsdp", scatter_dimension=0, tiled=True
        ).astype(jnp.float32),
        lax.psum_scatter(
            proj_weight_grad.astype(jnp.bfloat16), "fsdp", scatter_dimension=0, tiled=True
        ).astype(jnp.float32),
        lax.psum_scatter(
            proj_bias_grad.astype(jnp.bfloat16), "fsdp", scatter_dimension=0, tiled=True
        ).astype(jnp.float32),
        lax.psum_scatter(
            second_gain_grad.astype(jnp.bfloat16), "fsdp", scatter_dimension=0, tiled=True
        ).astype(jnp.float32),
        lax.psum_scatter(
            second_bias_grad.astype(jnp.bfloat16), "fsdp", scatter_dimension=0, tiled=True
        ).astype(jnp.float32),
        lax.psum_scatter(
            fc_weight_grad.astype(jnp.bfloat16), "fsdp", scatter_dimension=0, tiled=True
        ).astype(jnp.float32),
        lax.psum_scatter(
            fc_bias_grad.astype(jnp.bfloat16), "fsdp", scatter_dimension=0, tiled=True
        ).astype(jnp.float32),
        lax.psum_scatter(
            out_weight_grad.astype(jnp.bfloat16), "fsdp", scatter_dimension=0, tiled=True
        ).astype(jnp.float32),
        lax.psum_scatter(
            out_bias_grad.astype(jnp.bfloat16), "fsdp", scatter_dimension=0, tiled=True
        ).astype(jnp.float32),
    )
    summed = lax.psum(
        (
            owned[0],
            owned[1],
            owned[2],
            owned[3],
            owned[4],
            owned[5],
            owned[6],
            owned[7],
            owned[8],
            owned[9],
            owned[10],
            owned[11],
            owned[12],
        ),
        "ctx",
    )
    return (
        block_out.reshape(seq_count, block_rows, D),
        input_grad.reshape(seq_count, block_rows, D),
        summed[0],
        summed[1],
        summed[2],
        summed[3],
        summed[4],
        summed[5],
        summed[6],
        summed[7],
        summed[8],
        summed[9],
        summed[10],
        summed[11],
        summed[12],
    )


def solution(mesh):
    placed = (
        P("fsdp", "ctx", None),
        P("fsdp"),
        P("fsdp"),
        P("fsdp", None),
        P("fsdp"),
        P("fsdp"),
        P("fsdp", None),
        P("fsdp"),
        P("fsdp"),
        P("fsdp"),
        P("fsdp", None),
        P("fsdp"),
        P("fsdp", None),
        P("fsdp"),
        P("fsdp", "ctx", None),
    )
    return jax.shard_map(
        shards,
        mesh=mesh,
        in_specs=placed,
        out_specs=(
            P("fsdp", "ctx", None),
            P("fsdp", "ctx", None),
            P("fsdp"),
            P("fsdp"),
            P("fsdp", None),
            P("fsdp"),
            P("fsdp"),
            P("fsdp", None),
            P("fsdp"),
            P("fsdp"),
            P("fsdp"),
            P("fsdp", None),
            P("fsdp"),
            P("fsdp", None),
            P("fsdp"),
        ),
        check_vma=False,
    )
```

profile of v0, /device:TPU:0, one launch (start us, length us, event | category | flops | bytes accessed | tf_op | source)
XLA Modules:
  0.0 782.9 jit_solution(8197349530382373933)
XLA Ops:
  15.8 13.4 %all-reduce.19 = (bf16[768]{0:T(1024)(128)(2,1)S(1)}, bf16[768]{0:T(1024)(128)(2,1)S(1)}, bf16[768]{0:T(1024)(128)(2,1)S(1)}, bf16[768]{0:T(1024)(128)(2,1)S(1)}...) all-reduce(bf16[768]{0:T(1024)(128)(2,1)S(1)} %dynamic-update-slice, ...), channel_id=1, replica_groups=mesh['ctx'=8,'fsdp'=4] {'fsdp'}, use_global_device_ids=true, to_apply=%add.1 | all-reduce | flops 5376 | bytes 21504
  31.4 11.8 %all-gather.15.cloned.1.call-done = bf16[768,2304]{1,0:T(8,128)(2,1)} async-done(((bf16[192,2304]{1,0:T(8,128)(2,1)}), bf16[768,2304]{1,0:T(8,128)(2,1)}) %all-gather.15.cloned.1.call-update) | async-done | bytes 3538960 | tf_op jit(solution)/shard_map/all_gather | solution.py:83
  43.2 2.8 fusion.85
  49.5 5.2 all-gather.5
  55.7 35.5 %all-gather.25.cloned.1.call-done = bf16[1024,768]{1,0:T(8,128)(2,1)} async-done(((bf16[128,768]{1,0:T(8,128)(2,1)}), bf16[1024,768]{1,0:T(8,128)(2,1)}) %all-gather.25.cloned.1.call-update) | async-done | bytes 1572880 | tf_op jit(solution)/shard_map/all_gather | solution.py:115
  91.3 45.8 %all-gather.23.cloned.1.call-done = bf16[1024,768]{1,0:T(8,128)(2,1)} async-done(((bf16[128,768]{1,0:T(8,128)(2,1)}), bf16[1024,768]{1,0:T(8,128)(2,1)}) %all-gather.23.cloned.1.call-update) | async-done | bytes 1572880 | tf_op jit(solution)/shard_map/all_gather | solution.py:114
  137.1 13.5 %conditional.3 = (f32[1,12,128]{2,1,0:T(8,128)S(1)}, f32[1,12,128,64]{2,3,1,0:T(8,128)S(1)}, f32[1,12,128]{2,1,0:T(8,128)S(1)}) conditional(s32[]{:T(128)} %convert_element_type.215, () %tuple.32, (s32[]{:T(128)}, bf16[1,128,12,64]{1,3,2,0:T(8,128)(2,1)}, bf16[1,1024,768]{2,1,0:T(8,128)(2,1)}, bf16[1,1024,768]{2,1,0:T(8,128)(2,1)}) %tuple.106), branch_computations={%region_2.0_spmd.clone, %region_3.6_spmd.clone} | conditional | flops 423233152 | bytes 60988556 | solution.py:135
  145.6 4.9 fusion.32
  150.6 4.1 all-gather.17.cloned.1.call-done
  156.7 36.9 %all-gather.19.cloned.1.call-done = bf16[768,3072]{1,0:T(8,128)(2,1)} async-done(((bf16[192,3072]{1,0:T(8,128)(2,1)}), bf16[768,3072]{1,0:T(8,128)(2,1)}) %all-gather.19.cloned.1.call-update) | async-done | bytes 4718608 | tf_op jit(solution)/shard_map/all_gather | solution.py:149
  193.7 3.2 convolution_add_fusion
  196.9 35.7 %all-gather.21.cloned.1.call-done = bf16[3072,768]{1,0:T(8,128)(2,1)} async-done(((bf16[768,768]{1,0:T(8,128)(2,1)}), bf16[3072,768]{1,0:T(8,128)(2,1)}) %all-gather.21.cloned.1.call-update) | async-done | bytes 4718608 | tf_op jit(solution)/shard_map/all_gather | solution.py:151
  232.6 5.0 fusion.93
  244.4 4.9 convolution_convert_fusion.1
  249.6 3.8 convolution_convert_fusion
  255.2 17.2 %conditional.4 = (bf16[1,128,12,64]{1,3,2,0:T(8,128)(2,1)S(1)}) conditional(s32[]{:T(128)} %convert_element_type.215, () %tuple.34, (s32[]{:T(128)}, bf16[1,128,12,64]{1,3,2,0:T(8,128)(2,1)}, bf16[1,1024,768]{2,1,0:T(8,128)(2,1)}, f32[1,12,128]{2,1,0:T(8,128)}, bf16[1,128,12,64]{1,3,2,0:T(8,128)(2,1)}, /*index=5*/bf16[1,1024,768]{2,1,0:T(8,128)(2,1)}, ...), branch_computations={%region_11.12_spmd, %region_12.13_spmd} | conditional | flops 613744768 | bytes 25269316 | solution.py:257
  257.8 5.2 fusion.8
  265.8 6.6 fusion.5
  272.4 32.5 %all-gather.4 = f32[12,1024]{1,0:T(8,128)} all-gather(f32[12,128]{1,0:T(8,128)S(1)} %fusion.68), channel_id=6, replica_groups=mesh['ctx'=8,'fsdp'=4] {'ctx'}, dimensions={1}, use_global_device_ids=true | all-gather | bytes 55296 | tf_op jit(solution)/shard_map/all_gather | solution.py:191
  304.9 33.0 %all_gather.75 = f32[1,12,1024]{2,1,0:T(8,128)} all-gather(f32[1,12,128]{2,1,0:T(8,128)} %copy-done.22), channel_id=1, replica_groups=mesh['ctx'=8,'fsdp'=4] {'ctx'}, dimensions={2}, use_global_device_ids=true | all-gather | bytes 55296 | tf_op jit(solution)/shard_map/all_gather | solution.py:190
  338.0 23.5 %conditional.5 = (bf16[1,128,768]{1,2,0:T(8,128)(2,1)S(1)}, bf16[128,768]{0,1:T(8,128)(2,1)S(1)}) conditional(s32[]{:T(128)} %convert_element_type.242, () %tuple.36, (s32[]{:T(128)}, bf16[1,1024,768]{2,1,0:T(8,128)(2,1)}, bf16[128,768]{1,0:T(8,128)(2,1)S(1)}, f32[1,12,1024]{2,1,0:T(8,128)}, bf16[1,1024,768]{2,1,0:T(8,128)(2,1)}, ...), branch_computations={%region_13.14_spmd, %region_14.15_spmd} | conditional | flops 821362816 | bytes 33965132 | solution.py:221
  340.7 5.1 fusion.94
  348.7 8.3 %fusion.21 = bf16[12,128,64]{1,2,0:T(8,128)(2,1)S(1)} fusion(bf16[1024,12,64]{0,2,1:T(8,128)(2,1)} %bitcast.164, f32[12,1024,128]{2,1,0:T(8,128)} %fusion.94, f32[12,1024]{1,0:T(8,128)S(1)} %bitcast.189, f32[12,1024]{1,0:T(8,128)} %bitcast.190, pred[1024,128]{1,0:T(8,128)(4,1)S(1)} %iota_compare_fusion.1, bf16[1024,12,64]{0,2,1:T(8,128)(2,1)} %bitcast.176, ...), kind=kOutput, calls=%fused_computation.22 | convolution fusion | flops 412286976 | bytes 10059776 | tf_op jit(solution)/shard_map/cond/branch_1_fun/shqk,sqhd->skhd/dot_general | solution.py:213
  357.0 4.4 fusion.13
  361.5 3.3 convolution_convert_fusion.2
  369.7 4.1 fusion.88
  374.1 12.4 %all-reduce.18 = (bf16[768]{0:T(1024)(128)(2,1)S(1)}, bf16[768]{0:T(1024)(128)(2,1)S(1)}, bf16[768]{0:T(1024)(128)(2,1)S(1)}, bf16[768]{0:T(1024)(128)(2,1)S(1)}...) all-reduce(bf16[768]{0:T(1024)(128)(2,1)} %dynamic-update-slice.7, ...), channel_id=1, replica_groups=mesh['ctx'=8,'fsdp'=4] {'fsdp'}, use_global_device_ids=true, to_apply=%add.7 | all-reduce | flops 9984 | bytes 39936
  388.5 4.1 fusion.52
  392.6 10.9 %reduce-scatter.9.cloned.1.call-done = bf16[192,3072]{1,0:T(8,128)(2,1)} async-done(((bf16[768,3072]{1,0:T(8,128)(2,1)}), bf16[192,3072]{1,0:T(8,128)(2,1)}) %reduce-scatter.9.cloned.1.call-update) | async-done | bytes 1179664 | tf_op jit(solution)/shard_map/reduce_scatter | solution.py:310
  403.5 50.4 %reduce-scatter.11.cloned.1.call-done = bf16[768,768]{1,0:T(8,128)(2,1)} async-done(((bf16[3072,768]{1,0:T(8,128)(2,1)}), bf16[768,768]{1,0:T(8,128)(2,1)}) %reduce-scatter.11.cloned.1.call-update) | async-done | bytes 1179664 | tf_op jit(solution)/shard_map/reduce_scatter | solution.py:316
  453.9 43.0 %reduce-scatter.5.cloned.1.call-done = bf16[192,2304]{1,0:T(8,128)(2,1)} async-done(((bf16[768,2304]{1,0:T(8,128)(2,1)}), bf16[192,2304]{1,0:T(8,128)(2,1)}) %reduce-scatter.5.cloned.1.call-update) | async-done | bytes 884752 | tf_op jit(solution)/shard_map/reduce_scatter | solution.py:289
  497.0 279.1 %all-reduce.21 = (f32[192]{0:T(256)}, f32[192]{0:T(256)}, f32[192,2304]{1,0:T(8,128)}, f32[192]{0:T(256)}, f32[192]{0:T(256)}, /*index=5*/f32[192,768]{1,0:T(8,1...) all-reduce(f32[192]{0:T(256)S(1)} %get-tuple-element.212, ...), channel_id=1, replica_groups=mesh['ctx'=8,'fsdp'=4] {'ctx'}, use_global_device_ids=true, to_apply=%region_19.20 | all-reduce | flops 1771776 | bytes 10635264 | tf_op jit(solution)/shard_map/psum | solution.py:323
  (177 shorter events, 50.5 us)
Async XLA Ops:
  7.2 36.1 %all-gather.15.cloned.1.call-start = ((), (), s32[]{:S(2)}) async-start(), calls=%async_computation.4 | async-start | bytes 4423680 | tf_op jit(solution)/shard_map/all_gather | solution.py:83
  7.9 83.4 %all-gather.25.cloned.1.call-start = ((), (), s32[]{:S(2)}) async-start(), calls=%async_computation.13 | async-start | bytes 1769472 | tf_op jit(solution)/shard_map/all_gather | solution.py:115
  30.2 15.8 %copy-start.25 = (f32[128]{0:T(128)}, f32[128]{0:T(128)S(1)}, u32[]{:S(2)}) copy-start(f32[128]{0:T(128)S(1)} %broadcast_multiply_fusion.1) | copy-start | bytes 1540
  31.4 14.7 %copy-start.33 = (f32[128]{0:T(128)}, f32[128]{0:T(128)S(1)}, u32[]{:S(2)}) copy-start(f32[128]{0:T(128)S(1)} %fusion.63) | copy-start | bytes 1540
  31.4 14.7 %copy-start.28 = (f32[128]{0:T(128)}, f32[128]{0:T(128)S(1)}, u32[]{:S(2)}) copy-start(f32[128]{0:T(128)S(1)} %fusion.78) | copy-start | bytes 1540
  46.8 7.8 %copy-start.8 = (bf16[128,768]{1,0:T(8,128)(2,1)}, bf16[128,768]{1,0:T(8,128)(2,1)S(1)}, u32[]{:S(2)}) copy-start(bf16[128,768]{1,0:T(8,128)(2,1)S(1)} %get-tuple-element.195) | copy-start | bytes 589828
  46.9 90.2 %all-gather.23.cloned.1.call-start = ((), (), s32[]{:S(2)}) async-start(), calls=%async_computation.12 | async-start | bytes 1769472 | tf_op jit(solution)/shard_map/all_gather | solution.py:114
  47.6 107.1 %all-gather.17.cloned.1.call-start = ((), (), s32[]{:S(2)}) async-start(), calls=%async_computation.5 | async-start | bytes 1474560 | tf_op jit(solution)/shard_map/all_gather | solution.py:86
  48.2 145.5 %all-gather.19.cloned.1.call-start = ((), (), s32[]{:S(2)}) async-start(), calls=%async_computation.6 | async-start | bytes 5898240 | tf_op jit(solution)/shard_map/all_gather | solution.py:149
  48.8 183.8 %all-gather.21.cloned.1.call-start = ((), (), s32[]{:S(2)}) async-start(), calls=%async_computation.7 | async-start | bytes 5898240 | tf_op jit(solution)/shard_map/all_gather | solution.py:151
  49.4 288.5 %all-gather.27.cloned.1.call-start = ((), (), s32[]{:S(2)}) async-start(), calls=%async_computation.14 | async-start | bytes 1769472 | tf_op jit(solution)/shard_map/all_gather | solution.py:231
  55.5 282.4 %all-gather.29.cloned.1.call-start = ((), (), s32[]{:S(2)}) async-start(), calls=%async_computation.15 | async-start | bytes 1769472 | tf_op jit(solution)/shard_map/all_gather | solution.py:232
  137.1 17.7 %copy-start.2 = (bf16[1,128,768]{2,1,0:T(8,128)(2,1)S(1)}, bf16[1,128,768]{2,1,0:T(8,128)(2,1)}, u32[]{:S(2)}) copy-start(bf16[1,128,768]{2,1,0:T(8,128)(2,1)} %param.21) | copy-start | bytes 589828
  145.6 5.0 copy-start.17
  150.6 43.1 %copy-start.18 = (f32[1,12,128]{2,1,0:T(8,128)}, f32[1,12,128]{2,1,0:T(8,128)S(1)}, u32[]{:S(2)}) copy-start(f32[1,12,128]{2,1,0:T(8,128)S(1)} %get-tuple-element.81) | copy-start | bytes 18436
  150.6 43.1 %copy-start.22 = (f32[1,12,128]{2,1,0:T(8,128)}, f32[1,12,128]{2,1,0:T(8,128)S(1)}, u32[]{:S(2)}) copy-start(f32[1,12,128]{2,1,0:T(8,128)S(1)} %get-tuple-element.140) | copy-start | bytes 18436
  156.5 83.4 %copy-start.24 = (f32[128]{0:T(128)}, f32[128]{0:T(128)S(1)}, u32[]{:S(2)}) copy-start(f32[128]{0:T(128)S(1)} %broadcast_multiply_fusion) | copy-start | bytes 1540
  156.7 83.2 %copy-start.27 = (f32[128]{0:T(128)}, f32[128]{0:T(128)S(1)}, u32[]{:S(2)}) copy-start(f32[128]{0:T(128)S(1)} %fusion.79) | copy-start | bytes 1540
  193.7 38.9 %copy-start.10 = (bf16[1,128,768]{2,1,0:T(8,128)(2,1)S(1)}, bf16[1,128,768]{2,1,0:T(8,128)(2,1)}, u32[]{:S(2)}) copy-start(bf16[1,128,768]{2,1,0:T(8,128)(2,1)} %param.35) | copy-start | bytes 589828
  232.6 5.1 copy-start.1
  242.8 126.1 %reduce-scatter.7.cloned.1.call-start = ((), (), s32[]{:S(2)}) async-start(), calls=%async_computation.9 | async-start | bytes 1474560 | tf_op jit(solution)/shard_map/reduce_scatter | solution.py:298
  244.4 159.2 %reduce-scatter.9.cloned.1.call-start = ((), (), s32[]{:S(2)}) async-start(), calls=%async_computation.10 | async-start | bytes 5898240 | tf_op jit(solution)/shard_map/reduce_scatter | solution.py:310
  249.3 204.6 %reduce-scatter.11.cloned.1.call-start = ((), (), s32[]{:S(2)}) async-start(), calls=%async_computation.11 | async-start | bytes 5898240 | tf_op jit(solution)/shard_map/reduce_scatter | solution.py:316
  253.4 243.6 %reduce-scatter.5.cloned.1.call-start = ((), (), s32[]{:S(2)}) async-start(), calls=%async_computation.8 | async-start | bytes 4423680 | tf_op jit(solution)/shard_map/reduce_scatter | solution.py:289
  255.2 82.8 %copy-start.6 = (bf16[128,768]{1,0:T(8,128)(2,1)S(1)}, bf16[128,768]{1,0:T(8,128)(2,1)}, u32[]{:S(2)}) copy-start(bf16[128,768]{1,0:T(8,128)(2,1)} %get-tuple-element.194) | copy-start | bytes 589828
  255.2 82.8 %copy-start.7 = (bf16[128,768]{1,0:T(8,128)(2,1)S(1)}, bf16[128,768]{1,0:T(8,128)(2,1)}, u32[]{:S(2)}) copy-start(bf16[128,768]{1,0:T(8,128)(2,1)} %slice.23) | copy-start | bytes 589828
  337.9 23.6 %copy-start.26 = (f32[128]{0:T(128)S(1)}, f32[128]{0:T(128)}, u32[]{:S(2)}) copy-start(f32[128]{0:T(128)} %copy-done.25) | copy-start | bytes 1540
  337.9 23.6 %copy-start.29 = (f32[128]{0:T(128)S(1)}, f32[128]{0:T(128)}, u32[]{:S(2)}) copy-start(f32[128]{0:T(128)} %copy-done.28) | copy-start | bytes 1540
  348.7 8.3 %copy-start.21 = (f32[1,12,1024]{2,1,0:T(8,128)S(1)}, f32[1,12,1024]{2,1,0:T(8,128)}, u32[]{:S(2)}) copy-start(f32[1,12,1024]{2,1,0:T(8,128)} %get-tuple-element.56) | copy-start | bytes 147460 | tf_op jit(solution)/shard_map/cond
  369.7 4.4 copy-start.30
  369.7 17.2 %copy-start.11 = (bf16[1,128,768]{2,1,0:T(8,128)(2,1)S(1)}, bf16[1,128,768]{2,1,0:T(8,128)(2,1)}, u32[]{:S(2)}) copy-start(bf16[1,128,768]{2,1,0:T(8,128)(2,1)} %param.35) | copy-start | bytes 589828
  388.5 108.5 %copy-start.15 = (bf16[192,768]{1,0:T(8,128)(2,1)S(1)}, bf16[192,768]{1,0:T(8,128)(2,1)}, u32[]{:S(2)}) copy-start(bf16[192,768]{1,0:T(8,128)(2,1)} %reduce-scatter.7.cloned.1.call-done) | copy-start | bytes 884740
  (16 other events, 34.9 us)
Sparse Core Ops, SparseCore 0:
  9.6 33.6 all-gather.14
  47.0 44.2 all-gather.24
  94.0 42.9 all-gather.22
  138.5 16.2 all-gather.16
  156.2 37.4 all-gather.18
  195.1 37.4 all-gather.20
  234.8 44.3 all-gather.26
  281.3 43.2 all-gather.28
  327.8 24.7 reduce-scatter.6
  355.1 48.3 reduce-scatter.8
  406.0 47.8 reduce-scatter.10
  456.5 40.4 reduce-scatter.4
where the time goes:
time: 784 us; the launch traced here: 783 us
  blocking collectives  375 us (48%)
  waiting for transfers between devices  277 us (35%)
  matrix products  74.9 us (10%)
  local copies, waits for them, and re-layouts  28.5 us (4%)
  between operations  16.6 us (2%)
  other arithmetic  9.79 us (1%)
    psum x1, blocking collectives, shards(): lax.psum((owned[0], owned[1], owned[2], owned[3], owned[4], owned[5], own...  279 us
    reduce_scatter x1, waiting for transfers between devices, shards(): lax.psum_scatter(out_weight_grad.astype(jnp.bfloat16), 'fsdp', scatter_di...  50.4 us
    all_gather x1, waiting for transfers between devices, shards(): key_rows = lax.all_gather(key_flat, 'ctx', axis=1, tiled=True)  45.8 us
    reduce_scatter x1, waiting for transfers between devices, shards(): lax.psum_scatter(attn_weight_grad.astype(jnp.bfloat16), 'fsdp', scatter_d...  43 us
    all_gather x1, waiting for transfers between devices, shards(): lax.all_gather(fc_weight, 'fsdp', axis=0, tiled=True)  36.9 us
    all_gather x1, waiting for transfers between devices, shards(): lax.all_gather(out_weight, 'fsdp', axis=0, tiled=True)  35.7 us
    all_gather x1, waiting for transfers between devices, shards(): value_rows = lax.all_gather(value_flat, 'ctx', axis=1, tiled=True)  35.5 us
    all_gather x1, blocking collectives, shards(): lax.all_gather(log_totals, 'ctx', axis=2, tiled=True)  33 us
  transfers between devices with their start and end apart: 12, of which 9 were waited for; matrix products, arithmetic and copies ran while one was open for 14% of the time, Pallas kernels for 0%

commit v1 on v0

--- a/solution.py
+++ b/solution.py
@@ -111,7 +111,12 @@
         jnp.zeros((seq_count, H, block_rows, HD), jnp.float32),
     )
     offset = jnp.int32(0)
-    key_rows = lax.all_gather(key_flat, "ctx", axis=1, tiled=True)
+    ring = [key_flat]
+    for hop in range(7):
+        ring.append(lax.ppermute(ring[-1], "ctx", [(dev, (dev + 1) % 8) for dev in range(8)]))
+    key_rows = jnp.roll(
+        jnp.concatenate(ring[::-1], axis=1), (lax.axis_index("ctx") + 1) * ring[0].shape[1], axis=1
+    )
     value_rows = lax.all_gather(value_flat, "ctx", axis=1, tiled=True)
     row_count = key_rows.shape[1]
 

time: 784 us -> 796 us (1.015)
  local copies, waits for them, and re-layouts: 28.5 us -> 41.3 us
  waiting for transfers between devices: 277 us -> 265 us
    ppermute x0 -> x7, waiting for transfers between devices: none -> 60.5 us  [shards(): lax.ppermute(ring[-1], 'ctx', [(dev, (dev + 1) % 8) for dev in range(8)])]
    all_gather x1, waiting for transfers between devices: 35.5 us -> 0.01 us  [shards(): value_rows = lax.all_gather(value_flat, 'ctx', axis=1, tiled=True)]
    all_gather x1, waiting for transfers between devices: 36.9 us -> 8.09 us  [shards(): lax.all_gather(fc_weight, 'fsdp', axis=0, tiled=True)]
    all_gather x1, waiting for transfers between devices: 45.8 us -> 20.9 us  [shards(): lax.all_gather(key_flat, 'ctx', axis=1, tiled=True)]
    reduce_scatter x1, waiting for transfers between devices: 10.9 us -> 24.1 us  [shards(): lax.psum_scatter(fc_weight_grad.astype(jnp.bfloat16), 'fsdp', scatter_dim...]
    unnamed x74 -> x83, local copies, waits for them, and re-layouts: 11.2 us -> 22 us
  transfers between devices with their start and end apart: 12 -> 19, of which waited for: 9 -> 15; matrix products, arithmetic and copies ran while one was open for 14% -> 16% of each run, Pallas kernels for 0% -> 0%
where the time goes in v1:
time: 796 us; the launch traced here: 791 us
  blocking collectives  374 us (47%)
  waiting for transfers between devices  265 us (33%)
  matrix products  74.6 us (9%)
  local copies, waits for them, and re-layouts  41.3 us (5%)
  between operations  16.7 us (2%)
  other arithmetic  16.3 us (2%)
    psum x1, blocking collectives, shards(): lax.psum((owned[0], owned[1], owned[2], owned[3], owned[4], owned[5], own...  279 us
    ppermute x7, waiting for transfers between devices, shards(): lax.ppermute(ring[-1], 'ctx', [(dev, (dev + 1) % 8) for dev in range(8)])  60.5 us
    reduce_scatter x1, waiting for transfers between devices, shards(): lax.psum_scatter(out_weight_grad.astype(jnp.bfloat16), 'fsdp', scatter_di...  50.4 us
    reduce_scatter x1, waiting for transfers between devices, shards(): lax.psum_scatter(attn_weight_grad.astype(jnp.bfloat16), 'fsdp', scatter_d...  43 us
    all_gather x1, waiting for transfers between devices, shards(): lax.all_gather(out_weight, 'fsdp', axis=0, tiled=True)  35.7 us
    all_gather x1, blocking collectives, shards(): lax.all_gather(log_totals, 'ctx', axis=2, tiled=True)  32.7 us
    all_gather x1, blocking collectives, shards(): lax.all_gather(deltas, 'ctx', axis=2, tiled=True)  32.7 us
    unnamed x2, blocking collectives  24.8 us
  transfers between devices with their start and end apart: 19, of which 15 were waited for; matrix products, arithmetic and copies ran while one was open for 16% of the time, Pallas kernels for 0%

profile of v1, /device:TPU:0, one launch (start us, length us, event | category | flops | bytes accessed | tf_op | source)
XLA Modules:
  0.0 791.2 jit_solution(8442075585562435925)
XLA Ops:
  15.8 13.4 %all-reduce.19 = (bf16[768]{0:T(1024)(128)(2,1)S(1)}, bf16[768]{0:T(1024)(128)(2,1)S(1)}, bf16[768]{0:T(1024)(128)(2,1)S(1)}, bf16[768]{0:T(1024)(128)(2,1)S(1)}...) all-reduce(bf16[768]{0:T(1024)(128)(2,1)S(1)} %dynamic-update-slice, ...), channel_id=1, replica_groups=mesh['ctx'=8,'fsdp'=4] {'fsdp'}, use_global_device_ids=true, to_apply=%add.1 | all-reduce | flops 5376 | bytes 21504
  31.4 11.8 %all-gather.15.cloned.1.call-done = bf16[768,2304]{1,0:T(8,128)(2,1)} async-done(((bf16[192,2304]{1,0:T(8,128)(2,1)}), bf16[768,2304]{1,0:T(8,128)(2,1)}) %all-gather.15.cloned.1.call-update) | async-done | bytes 3538960 | tf_op jit(solution)/shard_map/all_gather | solution.py:83
  51.1 8.4 %collective-permute-done = bf16[1,128,768]{2,1,0:T(8,128)(2,1)S(1)} collective-permute-done((bf16[1,128,768]{2,1,0:T(8,128)(2,1)S(1)}, bf16[1,128,768]{2,1,0:T(8,128)(2,1)S(1)}, u32[]{:S(2)}, u32[]{:S(2)}) %collective-permute-start) | collective-permute-done | bytes 196640 | tf_op jit(solution)/shard_map/ppermute | solution.py:116
  59.5 12.1 %collective-permute-done.1 = bf16[1,128,768]{2,1,0:T(8,128)(2,1)S(1)} collective-permute-done((bf16[1,128,768]{2,1,0:T(8,128)(2,1)S(1)}, bf16[1,128,768]{2,1,0:T(8,128)(2,1)S(1)}, u32[]{:S(2)}, u32[]{:S(2)}) %collective-permute-start.1) | collective-permute-done | bytes 196640 | tf_op jit(solution)/shard_map/ppermute | solution.py:116
  71.6 10.0 %collective-permute-done.2 = bf16[1,128,768]{2,1,0:T(8,128)(2,1)S(1)} collective-permute-done((bf16[1,128,768]{2,1,0:T(8,128)(2,1)S(1)}, bf16[1,128,768]{2,1,0:T(8,128)(2,1)S(1)}, u32[]{:S(2)}, u32[]{:S(2)}) %collective-permute-start.2) | collective-permute-done | bytes 196640 | tf_op jit(solution)/shard_map/ppermute | solution.py:116
  81.6 11.0 %collective-permute-done.3 = bf16[1,128,768]{2,1,0:T(8,128)(2,1)S(1)} collective-permute-done((bf16[1,128,768]{2,1,0:T(8,128)(2,1)S(1)}, bf16[1,128,768]{2,1,0:T(8,128)(2,1)S(1)}, u32[]{:S(2)}, u32[]{:S(2)}) %collective-permute-start.3) | collective-permute-done | bytes 196640 | tf_op jit(solution)/shard_map/ppermute | solution.py:116
  92.6 9.8 %collective-permute-done.4 = bf16[1,128,768]{2,1,0:T(8,128)(2,1)S(1)} collective-permute-done((bf16[1,128,768]{2,1,0:T(8,128)(2,1)S(1)}, bf16[1,128,768]{2,1,0:T(8,128)(2,1)S(1)}, u32[]{:S(2)}, u32[]{:S(2)}) %collective-permute-start.4) | collective-permute-done | bytes 196640 | tf_op jit(solution)/shard_map/ppermute | solution.py:116
  102.4 8.5 %collective-permute-done.5 = bf16[1,128,768]{2,1,0:T(8,128)(2,1)S(1)} collective-permute-done((bf16[1,128,768]{2,1,0:T(8,128)(2,1)S(1)}, bf16[1,128,768]{2,1,0:T(8,128)(2,1)S(1)}, u32[]{:S(2)}, u32[]{:S(2)}) %collective-permute-start.5) | collective-permute-done | bytes 196640 | tf_op jit(solution)/shard_map/ppermute | solution.py:116
  111.5 5.2 all-gather.5
  130.4 15.7 %conditional.3 = (f32[1,12,128]{2,1,0:T(8,128)}, f32[1,12,128,64]{2,3,1,0:T(8,128)}, f32[1,12,128]{2,1,0:T(8,128)}) conditional(s32[]{:T(128)} %convert_element_type.218, () %tuple.43, (s32[]{:T(128)}, s32[]{:T(128)}, s32[]{:T(128)}, bf16[1,2048,768]{2,1,0:T(8,128)(2,1)}, bf16[1,128,12,64]{1,3,2,0:T(8,128)(2,1)S(1)}, ...), branch_computations={%region_2.3_spmd.clone, %region_3.6_spmd.clone} | conditional | flops 423233152 | bytes 68279592 | solution.py:140
  140.9 5.3 fusion.32
  149.2 8.1 %all-gather.19.cloned.1.call-done = bf16[768,3072]{1,0:T(8,128)(2,1)} async-done(((bf16[192,3072]{1,0:T(8,128)(2,1)}), bf16[768,3072]{1,0:T(8,128)(2,1)}) %all-gather.19.cloned.1.call-update) | async-done | bytes 4718608 | tf_op jit(solution)/shard_map/all_gather | solution.py:154
  160.5 35.7 %all-gather.21.cloned.1.call-done = bf16[3072,768]{1,0:T(8,128)(2,1)} async-done(((bf16[768,768]{1,0:T(8,128)(2,1)}), bf16[3072,768]{1,0:T(8,128)(2,1)}) %all-gather.21.cloned.1.call-update) | async-done | bytes 4718608 | tf_op jit(solution)/shard_map/all_gather | solution.py:156
  196.2 5.0 fusion.93
  210.2 4.4 convolution_convert_fusion.1
  221.5 20.9 %all-gather.25.cloned.1.call-done = bf16[1024,768]{1,0:T(8,128)(2,1)} async-done(((bf16[128,768]{1,0:T(8,128)(2,1)}), bf16[1024,768]{1,0:T(8,128)(2,1)}) %all-gather.25.cloned.1.call-update) | async-done | bytes 1572880 | tf_op jit(solution)/shard_map/all_gather | solution.py:267
  242.4 17.9 %conditional.4 = (bf16[1,128,12,64]{1,3,2,0:T(8,128)(2,1)S(1)}) conditional(s32[]{:T(128)} %convert_element_type.218, () %tuple.45, (s32[]{:T(128)}, bf16[1,128,12,64]{1,3,2,0:T(8,128)(2,1)}, bf16[1,1024,768]{2,1,0:T(8,128)(2,1)}, f32[1,12,128]{2,1,0:T(8,128)}, bf16[1,128,12,64]{1,3,2,0:T(8,128)(2,1)S(1)}, ...), branch_computations={%region_11.12_spmd, %region_12.13_spmd} | conditional | flops 613744768 | bytes 26817632 | solution.py:262
  245.2 5.1 fusion.8
  253.7 6.7 fusion.5
  260.4 32.7 %all-gather.4 = f32[12,1024]{1,0:T(8,128)} all-gather(f32[12,128]{1,0:T(8,128)S(1)} %fusion.68), channel_id=6, replica_groups=mesh['ctx'=8,'fsdp'=4] {'ctx'}, dimensions={1}, use_global_device_ids=true | all-gather | bytes 55296 | tf_op jit(solution)/shard_map/all_gather | solution.py:196
  293.0 32.7 %all_gather.74 = f32[1,12,1024]{2,1,0:T(8,128)} all-gather(f32[1,12,128]{2,1,0:T(8,128)} %get-tuple-element.248), channel_id=1, replica_groups=mesh['ctx'=8,'fsdp'=4] {'ctx'}, dimensions={2}, use_global_device_ids=true | all-gather | bytes 55296 | tf_op jit(solution)/shard_map/all_gather | solution.py:195
  325.8 7.6 all-gather.29.cloned.1.call-done
  333.4 23.5 %conditional.5 = (bf16[1,128,768]{1,2,0:T(8,128)(2,1)S(1)}, bf16[128,768]{0,1:T(8,128)(2,1)S(1)}) conditional(s32[]{:T(128)} %convert_element_type.245, () %tuple.47, (s32[]{:T(128)}, bf16[1,1024,768]{2,1,0:T(8,128)(2,1)}, bf16[128,768]{1,0:T(8,128)(2,1)S(1)}, f32[1,12,1024]{2,1,0:T(8,128)}, bf16[1,1024,768]{2,1,0:T(8,128)(2,1)}, ...), branch_computations={%region_13.14_spmd, %region_14.15_spmd} | conditional | flops 821362816 | bytes 33768496 | solution.py:226
  336.2 5.2 fusion.94
  344.3 8.2 %fusion.21 = bf16[12,128,64]{1,2,0:T(8,128)(2,1)S(1)} fusion(bf16[1024,12,64]{0,2,1:T(8,128)(2,1)} %bitcast.180, f32[12,1024,128]{2,1,0:T(8,128)} %fusion.94, f32[12,1024]{1,0:T(8,128)S(1)} %bitcast.205, f32[12,1024]{1,0:T(8,128)} %bitcast.206, pred[1024,128]{1,0:T(8,128)(4,1)S(1)} %iota_compare_fusion.1, bf16[1024,12,64]{0,2,1:T(8,128)(2,1)} %bitcast.195, ...), kind=kOutput, calls=%fused_computation.22 | convolution fusion | flops 412286976 | bytes 10059776 | tf_op jit(solution)/shard_map/cond/branch_1_fun/shqk,sqhd->skhd/dot_general | solution.py:218
  352.5 4.5 fusion.13
  369.8 11.4 %all-reduce.18 = (bf16[768]{0:T(1024)(128)(2,1)S(1)}, bf16[768]{0:T(1024)(128)(2,1)S(1)}, bf16[768]{0:T(1024)(128)(2,1)S(1)}, bf16[768]{0:T(1024)(128)(2,1)S(1)}...) all-reduce(bf16[768]{0:T(1024)(128)(2,1)} %dynamic-update-slice.7, ...), channel_id=1, replica_groups=mesh['ctx'=8,'fsdp'=4] {'fsdp'}, use_global_device_ids=true, to_apply=%add.7 | all-reduce | flops 9984 | bytes 39936
  383.3 4.2 fusion.52
  387.5 24.1 %reduce-scatter.9.cloned.1.call-done = bf16[192,3072]{1,0:T(8,128)(2,1)} async-done(((bf16[768,3072]{1,0:T(8,128)(2,1)}), bf16[192,3072]{1,0:T(8,128)(2,1)}) %reduce-scatter.9.cloned.1.call-update) | async-done | bytes 1179664 | tf_op jit(solution)/shard_map/reduce_scatter | solution.py:315
  411.6 50.4 %reduce-scatter.11.cloned.1.call-done = bf16[768,768]{1,0:T(8,128)(2,1)} async-done(((bf16[3072,768]{1,0:T(8,128)(2,1)}), bf16[768,768]{1,0:T(8,128)(2,1)}) %reduce-scatter.11.cloned.1.call-update) | async-done | bytes 1179664 | tf_op jit(solution)/shard_map/reduce_scatter | solution.py:321
  462.0 43.0 %reduce-scatter.5.cloned.1.call-done = bf16[192,2304]{1,0:T(8,128)(2,1)} async-done(((bf16[768,2304]{1,0:T(8,128)(2,1)}), bf16[192,2304]{1,0:T(8,128)(2,1)}) %reduce-scatter.5.cloned.1.call-update) | async-done | bytes 884752 | tf_op jit(solution)/shard_map/reduce_scatter | solution.py:294
  505.1 279.1 %all-reduce.21 = (f32[192]{0:T(256)}, f32[192]{0:T(256)}, f32[192,2304]{1,0:T(8,128)}, f32[192]{0:T(256)}, f32[192]{0:T(256)}, /*index=5*/f32[192,768]{1,0:T(8,1...) all-reduce(f32[192]{0:T(256)S(1)} %get-tuple-element.327, ...), channel_id=1, replica_groups=mesh['ctx'=8,'fsdp'=4] {'ctx'}, use_global_device_ids=true, to_apply=%region_19.20 | all-reduce | flops 1771776 | bytes 10635264 | tf_op jit(solution)/shard_map/psum | solution.py:328
  (203 shorter events, 89.9 us)
Async XLA Ops:
  7.2 36.1 %all-gather.15.cloned.1.call-start = ((), (), s32[]{:S(2)}) async-start(), calls=%async_computation.4 | async-start | bytes 4423680 | tf_op jit(solution)/shard_map/all_gather | solution.py:83
  7.9 122.5 %all-gather.23.cloned.1.call-start = ((), (), s32[]{:S(2)}) async-start(), calls=%async_computation.12 | async-start | bytes 1769472 | tf_op jit(solution)/shard_map/all_gather | solution.py:120
  30.2 16.6 %copy-start.23 = (f32[128]{0:T(128)}, f32[128]{0:T(128)S(1)}, u32[]{:S(2)}) copy-start(f32[128]{0:T(128)S(1)} %broadcast_multiply_fusion.1) | copy-start | bytes 1540
  31.4 15.4 %copy-start.31 = (f32[128]{0:T(128)}, f32[128]{0:T(128)S(1)}, u32[]{:S(2)}) copy-start(f32[128]{0:T(128)S(1)} %fusion.63) | copy-start | bytes 1540
  46.1 65.4 %copy-start.30 = (bf16[768]{0:T(1024)(128)(2,1)S(1)}, bf16[768]{0:T(1024)(128)(2,1)}, u32[]{:S(2)}) copy-start(bf16[768]{0:T(1024)(128)(2,1)} %param.32) | copy-start | bytes 4612
  46.8 71.3 %copy-start.6 = (bf16[128,768]{1,0:T(8,128)(2,1)}, bf16[128,768]{1,0:T(8,128)(2,1)S(1)}, u32[]{:S(2)}) copy-start(bf16[128,768]{1,0:T(8,128)(2,1)S(1)} %get-tuple-element.310) | copy-start | bytes 589828
  46.8 100.4 %all-gather.17.cloned.1.call-start = ((), (), s32[]{:S(2)}) async-start(), calls=%async_computation.5 | async-start | bytes 1474560 | tf_op jit(solution)/shard_map/all_gather | solution.py:86
  47.6 109.7 %all-gather.19.cloned.1.call-start = ((), (), s32[]{:S(2)}) async-start(), calls=%async_computation.6 | async-start | bytes 5898240 | tf_op jit(solution)/shard_map/all_gather | solution.py:154
  48.2 148.0 %all-gather.21.cloned.1.call-start = ((), (), s32[]{:S(2)}) async-start(), calls=%async_computation.7 | async-start | bytes 5898240 | tf_op jit(solution)/shard_map/all_gather | solution.py:156
  48.7 193.7 %all-gather.25.cloned.1.call-start = ((), (), s32[]{:S(2)}) async-start(), calls=%async_computation.13 | async-start | bytes 1769472 | tf_op jit(solution)/shard_map/all_gather | solution.py:267
  49.5 276.3 %all-gather.27.cloned.1.call-start = ((), (), s32[]{:S(2)}) async-start(), calls=%async_computation.14 | async-start | bytes 1769472 | tf_op jit(solution)/shard_map/all_gather | solution.py:236
  49.6 9.9 %collective-permute-start = (bf16[1,128,768]{2,1,0:T(8,128)(2,1)S(1)}, bf16[1,128,768]{2,1,0:T(8,128)(2,1)S(1)}, u32[]{:S(2)}, u32[]{:S(2)}) collective-permute-start(bf16[1,128,768]{2,1,0:T(8,128)(2,1)S(1)} %slice_bitcast_fusion), channel_id=1, source_target_pairs={{0,4},{4,8},{8,12},{12,16},{16,20},{20,24},{24,28},{28,0},{1,5},{5... | collective-permute-start | bytes 589832 | tf_op jit(solution)/shard_map/ppermute | solution.py:116
  59.5 12.1 %collective-permute-start.1 = (bf16[1,128,768]{2,1,0:T(8,128)(2,1)S(1)}, bf16[1,128,768]{2,1,0:T(8,128)(2,1)S(1)}, u32[]{:S(2)}, u32[]{:S(2)}) collective-permute-start(bf16[1,128,768]{2,1,0:T(8,128)(2,1)S(1)} %collective-permute-done), channel_id=1, source_target_pairs={{0,4},{4,8},{8,12},{12,16},{16,20},{20,24},{24,28},{28,0},{1,5},{5... | collective-permute-start | bytes 589832 | tf_op jit(solution)/shard_map/ppermute | solution.py:116
  71.6 10.0 %collective-permute-start.2 = (bf16[1,128,768]{2,1,0:T(8,128)(2,1)S(1)}, bf16[1,128,768]{2,1,0:T(8,128)(2,1)S(1)}, u32[]{:S(2)}, u32[]{:S(2)}) collective-permute-start(bf16[1,128,768]{2,1,0:T(8,128)(2,1)S(1)} %collective-permute-done.1), channel_id=1, source_target_pairs={{0,4},{4,8},{8,12},{12,16},{16,20},{20,24},{24,28},{28,0},{1,5},{5... | collective-permute-start | bytes 589832 | tf_op jit(solution)/shard_map/ppermute | solution.py:116
  81.6 11.0 %collective-permute-start.3 = (bf16[1,128,768]{2,1,0:T(8,128)(2,1)S(1)}, bf16[1,128,768]{2,1,0:T(8,128)(2,1)S(1)}, u32[]{:S(2)}, u32[]{:S(2)}) collective-permute-start(bf16[1,128,768]{2,1,0:T(8,128)(2,1)S(1)} %collective-permute-done.2), channel_id=1, source_target_pairs={{0,4},{4,8},{8,12},{12,16},{16,20},{20,24},{24,28},{28,0},{1,5},{5... | collective-permute-start | bytes 589832 | tf_op jit(solution)/shard_map/ppermute | solution.py:116
  92.6 9.8 %collective-permute-start.4 = (bf16[1,128,768]{2,1,0:T(8,128)(2,1)S(1)}, bf16[1,128,768]{2,1,0:T(8,128)(2,1)S(1)}, u32[]{:S(2)}, u32[]{:S(2)}) collective-permute-start(bf16[1,128,768]{2,1,0:T(8,128)(2,1)S(1)} %collective-permute-done.3), channel_id=1, source_target_pairs={{0,4},{4,8},{8,12},{12,16},{16,20},{20,24},{24,28},{28,0},{1,5},{5... | collective-permute-start | bytes 589832 | tf_op jit(solution)/shard_map/ppermute | solution.py:116
  102.4 8.5 %collective-permute-start.5 = (bf16[1,128,768]{2,1,0:T(8,128)(2,1)S(1)}, bf16[1,128,768]{2,1,0:T(8,128)(2,1)S(1)}, u32[]{:S(2)}, u32[]{:S(2)}) collective-permute-start(bf16[1,128,768]{2,1,0:T(8,128)(2,1)S(1)} %collective-permute-done.4), channel_id=1, source_target_pairs={{0,4},{4,8},{8,12},{12,16},{16,20},{20,24},{24,28},{28,0},{1,5},{5... | collective-permute-start | bytes 589832 | tf_op jit(solution)/shard_map/ppermute | solution.py:116
  110.9 8.4 %collective-permute-start.6 = (bf16[1,128,768]{2,1,0:T(8,128)(2,1)S(1)}, bf16[1,128,768]{2,1,0:T(8,128)(2,1)S(1)}, u32[]{:S(2)}, u32[]{:S(2)}) collective-permute-start(bf16[1,128,768]{2,1,0:T(8,128)(2,1)S(1)} %collective-permute-done.5), channel_id=1, source_target_pairs={{0,4},{4,8},{8,12},{12,16},{16,20},{20,24},{24,28},{28,0},{1,5},{5... | collective-permute-start | bytes 589832 | tf_op jit(solution)/shard_map/ppermute | solution.py:116
  118.2 215.3 %all-gather.29.cloned.1.call-start = ((), (), s32[]{:S(2)}) async-start(), calls=%async_computation.15 | async-start | bytes 1769472 | tf_op jit(solution)/shard_map/all_gather | solution.py:237
  130.4 16.8 %copy-start.2 = (bf16[1,128,768]{2,1,0:T(8,128)(2,1)S(1)}, bf16[1,128,768]{2,1,0:T(8,128)(2,1)}, u32[]{:S(2)}) copy-start(bf16[1,128,768]{2,1,0:T(8,128)(2,1)} %param.21) | copy-start | bytes 589828
  149.0 52.3 %copy-start.22 = (f32[128]{0:T(128)}, f32[128]{0:T(128)S(1)}, u32[]{:S(2)}) copy-start(f32[128]{0:T(128)S(1)} %broadcast_multiply_fusion) | copy-start | bytes 1540
  149.2 52.1 %copy-start.25 = (f32[128]{0:T(128)}, f32[128]{0:T(128)S(1)}, u32[]{:S(2)}) copy-start(f32[128]{0:T(128)S(1)} %fusion.79) | copy-start | bytes 1540
  157.3 38.9 %copy-start.10 = (bf16[1,128,768]{2,1,0:T(8,128)(2,1)S(1)}, bf16[1,128,768]{2,1,0:T(8,128)(2,1)}, u32[]{:S(2)}) copy-start(bf16[1,128,768]{2,1,0:T(8,128)(2,1)} %param.35) | copy-start | bytes 589828
  207.2 156.9 %reduce-scatter.7.cloned.1.call-start = ((), (), s32[]{:S(2)}) async-start(), calls=%async_computation.9 | async-start | bytes 1474560 | tf_op jit(solution)/shard_map/reduce_scatter | solution.py:303
  209.7 201.9 %reduce-scatter.9.cloned.1.call-start = ((), (), s32[]{:S(2)}) async-start(), calls=%async_computation.10 | async-start | bytes 5898240 | tf_op jit(solution)/shard_map/reduce_scatter | solution.py:315
  214.6 247.4 %reduce-scatter.11.cloned.1.call-start = ((), (), s32[]{:S(2)}) async-start(), calls=%async_computation.11 | async-start | bytes 5898240 | tf_op jit(solution)/shard_map/reduce_scatter | solution.py:321
  219.4 285.7 %reduce-scatter.5.cloned.1.call-start = ((), (), s32[]{:S(2)}) async-start(), calls=%async_computation.8 | async-start | bytes 4423680 | tf_op jit(solution)/shard_map/reduce_scatter | solution.py:294
  242.4 91.0 %copy-start.5 = (bf16[128,768]{1,0:T(8,128)(2,1)S(1)}, bf16[128,768]{1,0:T(8,128)(2,1)}, u32[]{:S(2)}) copy-start(bf16[128,768]{1,0:T(8,128)(2,1)} %get-tuple-element.309) | copy-start | bytes 589828
  242.4 91.0 %copy-start.7 = (bf16[128,768]{1,0:T(8,128)(2,1)S(1)}, bf16[128,768]{1,0:T(8,128)(2,1)}, u32[]{:S(2)}) copy-start(bf16[128,768]{1,0:T(8,128)(2,1)} %slice.23) | copy-start | bytes 589828
  333.4 23.6 %copy-start.24 = (f32[128]{0:T(128)S(1)}, f32[128]{0:T(128)}, u32[]{:S(2)}) copy-start(f32[128]{0:T(128)} %copy-done.23) | copy-start | bytes 1540
  333.4 23.6 %copy-start.27 = (f32[128]{0:T(128)S(1)}, f32[128]{0:T(128)}, u32[]{:S(2)}) copy-start(f32[128]{0:T(128)} %copy-done.26) | copy-start | bytes 1540
  383.3 121.8 %copy-start.20 = (bf16[192,768]{1,0:T(8,128)(2,1)S(1)}, bf16[192,768]{1,0:T(8,128)(2,1)}, u32[]{:S(2)}) copy-start(bf16[192,768]{1,0:T(8,128)(2,1)} %reduce-scatter.7.cloned.1.call-done) | copy-start | bytes 884740
  (20 other events, 82.5 us)
Sparse Core Ops, SparseCore 0:
  9.6 33.6 all-gather.14
  46.9 51.2 all-gather.22
  99.8 18.5 all-gather.16
  119.8 37.4 all-gather.18
  158.7 37.4 all-gather.20
  198.2 44.1 all-gather.24
  244.6 43.3 all-gather.26
  290.2 43.1 all-gather.28
  336.6 24.5 reduce-scatter.6
  363.7 47.8 reduce-scatter.8
  414.1 47.8 reduce-scatter.10
  464.6 40.4 reduce-scatter.4
